TPU v7x, 256 devices: a whole 4x4x8 slice. The times are simulated.
256 devices in a mesh: req: 16 (over x_hi, y, core), ctx: 16 (over x_lo, z).
Axes of the slice: x: 4 (x_hi: 2, x_lo: 2; x = x_hi * 2 + x_lo), y: 4, z: 8, core: 2. Of those that a mesh axis runs over, the one named last changes fastest.
Arguments:
- queries: bfloat16 [1024, 8192], P(('req', 'ctx')), parts along dimension 0, may hold values from -15 to 15
- new_keys: bfloat16 [1024, 512], P(('req', 'ctx')), parts along dimension 0, may hold values from -9 to 9
- new_values: bfloat16 [1024, 512], P(('req', 'ctx')), parts along dimension 0, may hold values from -6 to 6
- cache_keys: bfloat16 [524288, 512], P(('req', 'ctx')), parts along dimension 0, may hold values from -6 to 6
- cache_values: bfloat16 [524288, 512], P(('req', 'ctx')), parts along dimension 0, may hold values from -6 to 6
- cache_length: int32 [16], P('req'), parts along dimension 0, may hold values from 8192 to 32767
- page_table: int32 [4096], P('req'), parts along dimension 0, may hold values from 0 to 255, each once
Outputs:
- attended: bfloat16 [1024, 8192], P(('req', 'ctx')), parts along dimension 0
There are 16 independent parts, one for each index of `req`. A program takes and returns all parts, laid end to end along the dimension named above; each array names one. Nothing has to cross between parts.
Inputs may be any that keep to these rules, and one draw needn't show every extreme that they name: A permutation: logical page p lies in physical rows page_table[p] * 128 to page_table[p] * 128 + 127.
All inputs are finite; a program needn't handle non-finite values.
Results may differ from a plain program's by a relative error of at most 0.004.
Values may be sent and summed in bfloat16 or wider, within the bound.
No kernel may reach another device: no remote copies, remote signals or barrier semaphores. Data moves between devices by JAX's collectives and lax.ppermute only.
A program may use at most 64 MiB of HBM per device.

v0:
```python
import jax
import jax.numpy as jnp
from jax import lax
from jax.sharding import PartitionSpec as P

KVH = 4
HD = 128
PAGE = 128
floor_score = -1e30


def from_behind(x, axis, by):
    devices = lax.axis_size(axis)
    return lax.ppermute(x, axis, [(i, (i + by) % devices) for i in range(devices)])


def attend(queries, query_pos, keys, values, key_pos, key_ok):
    rows = queries.shape[0]
    heads = queries.shape[1] // HD
    grouped = queries.reshape(rows, KVH, heads // KVH, HD)
    key_count = keys.shape[0]
    keys_grouped = keys.reshape(key_count, KVH, HD)
    values_grouped = values.reshape(key_count, KVH, HD)
    scores = jnp.einsum(
        "rkgd,nkd->rkgn", grouped, keys_grouped, preferred_element_type=jnp.float32
    ) * HD ** (-0.5)
    allowed = key_ok[None, :] & (key_pos[None, :] <= query_pos[:, None])
    allowed = allowed[:, None, None, :]
    scores = jnp.where(allowed, scores, floor_score)
    top = jnp.max(scores, axis=3)
    weights = jnp.where(allowed, jnp.exp(scores - top[..., None]), 0.0)
    total = jnp.sum(weights, axis=3)
    mixed = jnp.einsum(
        "rkgn,nkd->rkgd",
        weights.astype(jnp.bfloat16),
        values_grouped,
        preferred_element_type=jnp.float32,
    )
    return (mixed.reshape(rows, heads * HD), top.reshape(rows, heads), total.reshape(rows, heads))


def combine(first, second):
    mixed_first, top_first, total_first = first
    mixed_second, top_second, total_second = second
    rows, heads = top_first.shape
    top = jnp.maximum(top_first, top_second)
    factor_first = jnp.exp(top_first - top)
    factor_second = jnp.exp(top_second - top)
    mixed = (
        mixed_first.reshape(rows, heads, HD) * factor_first[..., None]
        + mixed_second.reshape(rows, heads, HD) * factor_second[..., None]
    )
    return (
        mixed.reshape(rows, heads * HD),
        top,
        factor_first * total_first + factor_second * total_second,
    )


def empty_state(rows, heads):
    return (
        jnp.zeros((rows, heads * HD), jnp.float32),
        jnp.full((rows, heads), floor_score, jnp.float32),
        jnp.zeros((rows, heads), jnp.float32),
    )


def settle(moved):
    return (moved[0], moved[1], moved[2], moved[3])


def local(queries, new_keys, new_values, cache_keys, cache_values, cache_length, page_table):
    count = lax.axis_size("ctx")
    device = lax.axis_index("ctx")
    rows = queries.shape[0]
    heads = queries.shape[1] // HD
    local_pages = cache_keys.shape[0] // PAGE
    length = cache_length[0]
    slots = device * local_pages + lax.iota(jnp.int32, local_pages)
    hits = (page_table[:, None] == slots[None, :]).astype(jnp.int32)
    logical = jnp.sum(hits * lax.iota(jnp.int32, page_table.shape[0])[:, None], axis=0)
    cache_pos = (logical[:, None] * PAGE + lax.iota(jnp.int32, PAGE)[None, :]).reshape(-1)
    cache_live = cache_pos < length
    own_pos = length + device * rows + lax.iota(jnp.int32, rows)

    def attend_cache(held, positions):
        return attend(held, positions, cache_keys, cache_values, cache_pos, cache_live)

    keys_piece = lax.all_gather(new_keys, "ctx", axis=0, tiled=True)
    values_piece = lax.all_gather(new_values, "ctx", axis=0, tiled=True)
    piece_rows = keys_piece.shape[0]
    key_pos = length + lax.iota(jnp.int32, piece_rows)
    span_state = combine(
        empty_state(rows, heads),
        attend(queries, own_pos, keys_piece, values_piece, key_pos, jnp.ones((piece_rows,), bool)),
    )

    def hop_one(step, carry):
        held = carry[0]
        source = (device - step) % count
        positions = length + source * rows + lax.iota(jnp.int32, rows)
        state = combine(carry[1:4], attend_cache(held, positions))
        return settle(from_behind((held,) + state, "ctx", 1))

    final = lax.fori_loop(0, count, hop_one, (queries,) + empty_state(rows, heads))
    cycle_state = final[1:4]
    mixed, top, total = combine(cycle_state, span_state)
    result = mixed.reshape(rows, heads, HD) / total[..., None]
    return result.reshape(rows, heads * HD).astype(jnp.bfloat16)


def solution(mesh):
    in_specs = (
        P(("req", "ctx"), None),
        P(("req", "ctx"), None),
        P(("req", "ctx"), None),
        P(("req", "ctx"), None),
        P(("req", "ctx"), None),
        P("req"),
        P("req"),
    )
    out_specs = P(("req", "ctx"), None)
    return jax.shard_map(local, mesh=mesh, in_specs=in_specs, out_specs=out_specs, check_vma=False)
```

profile of v0, /device:TPU:2, one launch (start us, length us, event | category | flops | bytes accessed | tf_op | source)
XLA Modules:
  0.0 324.2 jit_solution(2116719299812118511)
XLA Ops:
  2.5 35.9 %all-gather = bf16[16,4,512]{2,1,0:T(4,128)(2,1)S(1)} all-gather(bf16[1,4,512]{2,1,0:T(4,128)(2,1)} %bitcast.139), channel_id=1, replica_groups=mesh['req'=16,'ctx'=16] {'ctx'}, dimensions={0}, use_global_device_ids=true | all-gather | bytes 69632 | tf_op jit(solution)/shard_map/all_gather | solution.py:89
  38.4 30.2 %all-gather.1 = bf16[16,4,512]{2,1,0:T(4,128)(2,1)S(1)} all-gather(bf16[1,4,512]{2,1,0:T(4,128)(2,1)} %bitcast.140), channel_id=1, replica_groups=mesh['req'=16,'ctx'=16] {'ctx'}, dimensions={0}, use_global_device_ids=true | all-gather | bytes 69632 | tf_op jit(solution)/shard_map/all_gather | solution.py:90
  69.5 4.1 %reshape.248 = bf16[2048,4,128]{2,1,0:T(4,128)(2,1)} reshape(bf16[2048,512]{1,0:T(8,128)(2,1)} %param.12) | data formatting | bytes 4194304 | tf_op jit(solution)/shard_map/while/body/eval_jaxpr/reshape | solution.py:22
  75.7 247.0 %while.24 = (s32[]{:T(128)}, bf16[4,8192]{1,0:T(4,128)(2,1)S(1)}, f32[4,8192]{1,0:T(4,128)S(1)}, f32[4,64]{1,0:T(4,128)S(1)}, f32[4,64]{1,0:T(4,128)S(1)}, /*ind...) while((s32[]{:T(128)}, bf16[4,8192]{1,0:T(4,128)(2,1)S(1)}, ...), condition=%wide.wide.region_4.5_spmd.clone.clone, body=%wide.wide.region_1.4_spmd.clone.clone.sunk | while | flops 273275904 | bytes 21383824 | solution.py:105
  77.4 2.5 fusion.68
  85.1 6.5 %collective-permute-done.2 = f32[4,64]{1,0:T(4,128)S(1)} collective-permute-done((f32[4,64]{1,0:T(4,128)S(1)}, f32[4,64]{1,0:T(4,128)S(1)}, u32[]{:S(2)}, u32[]{:S(2)}) %collective-permute-start.2) | collective-permute-done | bytes 1056 | tf_op jit(solution)/shard_map/while/body/eval_jaxpr/ppermute | solution.py:14
  99.5 3.5 %collective-permute-start.3 = (f32[4,64]{1,0:T(4,128)S(1)}, f32[4,64]{1,0:T(4,128)S(1)}, u32[]{:S(2)}, u32[]{:S(2)}) collective-permute-start(f32[4,64]{1,0:T(4,128)S(1)} %get-tuple-element.509), channel_id=1, source_target_pairs={{0,1},{1,2},{2,3},{3,4},{4,5},{5,6},{6,7},{7,8},{8,9},{9,10},{10,1... | collective-permute-start | bytes 3080 | tf_op jit(solution)/shard_map/while/body/eval_jaxpr/ppermute | solution.py:14
  103.0 3.8 %collective-permute-done.2 = f32[4,64]{1,0:T(4,128)S(1)} collective-permute-done((f32[4,64]{1,0:T(4,128)S(1)}, f32[4,64]{1,0:T(4,128)S(1)}, u32[]{:S(2)}, u32[]{:S(2)}) %collective-permute-start.2) | collective-permute-done | bytes 1056 | tf_op jit(solution)/shard_map/while/body/eval_jaxpr/ppermute | solution.py:14
  118.0 3.8 %collective-permute-done.2 = f32[4,64]{1,0:T(4,128)S(1)} collective-permute-done((f32[4,64]{1,0:T(4,128)S(1)}, f32[4,64]{1,0:T(4,128)S(1)}, u32[]{:S(2)}, u32[]{:S(2)}) %collective-permute-start.2) | collective-permute-done | bytes 1056 | tf_op jit(solution)/shard_map/while/body/eval_jaxpr/ppermute | solution.py:14
  132.8 4.6 %collective-permute-done.2 = f32[4,64]{1,0:T(4,128)S(1)} collective-permute-done((f32[4,64]{1,0:T(4,128)S(1)}, f32[4,64]{1,0:T(4,128)S(1)}, u32[]{:S(2)}, u32[]{:S(2)}) %collective-permute-start.2) | collective-permute-done | bytes 1056 | tf_op jit(solution)/shard_map/while/body/eval_jaxpr/ppermute | solution.py:14
  147.8 4.6 %collective-permute-done.2 = f32[4,64]{1,0:T(4,128)S(1)} collective-permute-done((f32[4,64]{1,0:T(4,128)S(1)}, f32[4,64]{1,0:T(4,128)S(1)}, u32[]{:S(2)}, u32[]{:S(2)}) %collective-permute-start.2) | collective-permute-done | bytes 1056 | tf_op jit(solution)/shard_map/while/body/eval_jaxpr/ppermute | solution.py:14
  162.9 4.6 %collective-permute-done.2 = f32[4,64]{1,0:T(4,128)S(1)} collective-permute-done((f32[4,64]{1,0:T(4,128)S(1)}, f32[4,64]{1,0:T(4,128)S(1)}, u32[]{:S(2)}, u32[]{:S(2)}) %collective-permute-start.2) | collective-permute-done | bytes 1056 | tf_op jit(solution)/shard_map/while/body/eval_jaxpr/ppermute | solution.py:14
  177.9 4.6 %collective-permute-done.2 = f32[4,64]{1,0:T(4,128)S(1)} collective-permute-done((f32[4,64]{1,0:T(4,128)S(1)}, f32[4,64]{1,0:T(4,128)S(1)}, u32[]{:S(2)}, u32[]{:S(2)}) %collective-permute-start.2) | collective-permute-done | bytes 1056 | tf_op jit(solution)/shard_map/while/body/eval_jaxpr/ppermute | solution.py:14
  193.5 4.1 %collective-permute-done.2 = f32[4,64]{1,0:T(4,128)S(1)} collective-permute-done((f32[4,64]{1,0:T(4,128)S(1)}, f32[4,64]{1,0:T(4,128)S(1)}, u32[]{:S(2)}, u32[]{:S(2)}) %collective-permute-start.2) | collective-permute-done | bytes 1056 | tf_op jit(solution)/shard_map/while/body/eval_jaxpr/ppermute | solution.py:14
  208.5 4.1 %collective-permute-done.2 = f32[4,64]{1,0:T(4,128)S(1)} collective-permute-done((f32[4,64]{1,0:T(4,128)S(1)}, f32[4,64]{1,0:T(4,128)S(1)}, u32[]{:S(2)}, u32[]{:S(2)}) %collective-permute-start.2) | collective-permute-done | bytes 1056 | tf_op jit(solution)/shard_map/while/body/eval_jaxpr/ppermute | solution.py:14
  223.6 4.0 %collective-permute-done.2 = f32[4,64]{1,0:T(4,128)S(1)} collective-permute-done((f32[4,64]{1,0:T(4,128)S(1)}, f32[4,64]{1,0:T(4,128)S(1)}, u32[]{:S(2)}, u32[]{:S(2)}) %collective-permute-start.2) | collective-permute-done | bytes 1056 | tf_op jit(solution)/shard_map/while/body/eval_jaxpr/ppermute | solution.py:14
  236.2 2.5 collective-permute-start.3
  238.8 4.9 %collective-permute-done.2 = f32[4,64]{1,0:T(4,128)S(1)} collective-permute-done((f32[4,64]{1,0:T(4,128)S(1)}, f32[4,64]{1,0:T(4,128)S(1)}, u32[]{:S(2)}, u32[]{:S(2)}) %collective-permute-start.2) | collective-permute-done | bytes 1056 | tf_op jit(solution)/shard_map/while/body/eval_jaxpr/ppermute | solution.py:14
  251.3 3.3 %collective-permute-start.3 = (f32[4,64]{1,0:T(4,128)S(1)}, f32[4,64]{1,0:T(4,128)S(1)}, u32[]{:S(2)}, u32[]{:S(2)}) collective-permute-start(f32[4,64]{1,0:T(4,128)S(1)} %get-tuple-element.509), channel_id=1, source_target_pairs={{0,1},{1,2},{2,3},{3,4},{4,5},{5,6},{6,7},{7,8},{8,9},{9,10},{10,1... | collective-permute-start | bytes 3080 | tf_op jit(solution)/shard_map/while/body/eval_jaxpr/ppermute | solution.py:14
  254.6 6.2 %collective-permute-done.2 = f32[4,64]{1,0:T(4,128)S(1)} collective-permute-done((f32[4,64]{1,0:T(4,128)S(1)}, f32[4,64]{1,0:T(4,128)S(1)}, u32[]{:S(2)}, u32[]{:S(2)}) %collective-permute-start.2) | collective-permute-done | bytes 1056 | tf_op jit(solution)/shard_map/while/body/eval_jaxpr/ppermute | solution.py:14
  270.2 7.0 %collective-permute-done.2 = f32[4,64]{1,0:T(4,128)S(1)} collective-permute-done((f32[4,64]{1,0:T(4,128)S(1)}, f32[4,64]{1,0:T(4,128)S(1)}, u32[]{:S(2)}, u32[]{:S(2)}) %collective-permute-start.2) | collective-permute-done | bytes 1056 | tf_op jit(solution)/shard_map/while/body/eval_jaxpr/ppermute | solution.py:14
  285.2 7.5 %collective-permute-done.2 = f32[4,64]{1,0:T(4,128)S(1)} collective-permute-done((f32[4,64]{1,0:T(4,128)S(1)}, f32[4,64]{1,0:T(4,128)S(1)}, u32[]{:S(2)}, u32[]{:S(2)}) %collective-permute-start.2) | collective-permute-done | bytes 1056 | tf_op jit(solution)/shard_map/while/body/eval_jaxpr/ppermute | solution.py:14
  301.8 5.9 %collective-permute-done.2 = f32[4,64]{1,0:T(4,128)S(1)} collective-permute-done((f32[4,64]{1,0:T(4,128)S(1)}, f32[4,64]{1,0:T(4,128)S(1)}, u32[]{:S(2)}, u32[]{:S(2)}) %collective-permute-start.2) | collective-permute-done | bytes 1056 | tf_op jit(solution)/shard_map/while/body/eval_jaxpr/ppermute | solution.py:14
  317.6 5.2 %collective-permute-done.2 = f32[4,64]{1,0:T(4,128)S(1)} collective-permute-done((f32[4,64]{1,0:T(4,128)S(1)}, f32[4,64]{1,0:T(4,128)S(1)}, u32[]{:S(2)}, u32[]{:S(2)}) %collective-permute-start.2) | collective-permute-done | bytes 1056 | tf_op jit(solution)/shard_map/while/body/eval_jaxpr/ppermute | solution.py:14
  (441 shorter events, 147.7 us)
Async XLA Ops:
  82.9 8.8 %collective-permute-start.1 = (f32[4,8192]{1,0:T(4,128)S(1)}, f32[4,8192]{1,0:T(4,128)S(1)}, u32[]{:S(2)}, u32[]{:S(2)}) collective-permute-start(f32[4,8192]{1,0:T(4,128)S(1)} %fusion.71), channel_id=1, source_target_pairs={{0,1},{1,2},{2,3},{3,4},{4,5},{5,6},{6,7},{7,8},{8,9},{9,10},{10,1... | collective-permute-start | bytes 393224 | tf_op jit(solution)/shard_map/while/body/eval_jaxpr/ppermute | solution.py:14
  98.9 8.0 %collective-permute-start.1 = (f32[4,8192]{1,0:T(4,128)S(1)}, f32[4,8192]{1,0:T(4,128)S(1)}, u32[]{:S(2)}, u32[]{:S(2)}) collective-permute-start(f32[4,8192]{1,0:T(4,128)S(1)} %fusion.71), channel_id=1, source_target_pairs={{0,1},{1,2},{2,3},{3,4},{4,5},{5,6},{6,7},{7,8},{8,9},{9,10},{10,1... | collective-permute-start | bytes 393224 | tf_op jit(solution)/shard_map/while/body/eval_jaxpr/ppermute | solution.py:14
  113.9 8.5 %collective-permute-start.1 = (f32[4,8192]{1,0:T(4,128)S(1)}, f32[4,8192]{1,0:T(4,128)S(1)}, u32[]{:S(2)}, u32[]{:S(2)}) collective-permute-start(f32[4,8192]{1,0:T(4,128)S(1)} %fusion.71), channel_id=1, source_target_pairs={{0,1},{1,2},{2,3},{3,4},{4,5},{5,6},{6,7},{7,8},{8,9},{9,10},{10,1... | collective-permute-start | bytes 393224 | tf_op jit(solution)/shard_map/while/body/eval_jaxpr/ppermute | solution.py:14
  114.0 8.4 %collective-permute-start = (bf16[4,8192]{1,0:T(4,128)(2,1)S(1)}, bf16[4,8192]{1,0:T(4,128)(2,1)S(1)}, u32[]{:S(2)}, u32[]{:S(2)}) collective-permute-start(bf16[4,8192]{1,0:T(4,128)(2,1)S(1)} %copy.160), channel_id=1, source_target_pairs={{0,1},{1,2},{2,3},{3,4},{4,5},{5,6},{6,7},{7,8},{8,9},{9,10},{10,1... | collective-permute-start | bytes 196616 | tf_op jit(solution)/shard_map/while/body/eval_jaxpr/ppermute | solution.py:14
  129.5 7.9 %collective-permute-start.1 = (f32[4,8192]{1,0:T(4,128)S(1)}, f32[4,8192]{1,0:T(4,128)S(1)}, u32[]{:S(2)}, u32[]{:S(2)}) collective-permute-start(f32[4,8192]{1,0:T(4,128)S(1)} %fusion.71), channel_id=1, source_target_pairs={{0,1},{1,2},{2,3},{3,4},{4,5},{5,6},{6,7},{7,8},{8,9},{9,10},{10,1... | collective-permute-start | bytes 393224 | tf_op jit(solution)/shard_map/while/body/eval_jaxpr/ppermute | solution.py:14
  144.6 7.9 %collective-permute-start.1 = (f32[4,8192]{1,0:T(4,128)S(1)}, f32[4,8192]{1,0:T(4,128)S(1)}, u32[]{:S(2)}, u32[]{:S(2)}) collective-permute-start(f32[4,8192]{1,0:T(4,128)S(1)} %fusion.71), channel_id=1, source_target_pairs={{0,1},{1,2},{2,3},{3,4},{4,5},{5,6},{6,7},{7,8},{8,9},{9,10},{10,1... | collective-permute-start | bytes 393224 | tf_op jit(solution)/shard_map/while/body/eval_jaxpr/ppermute | solution.py:14
  159.6 7.9 %collective-permute-start.1 = (f32[4,8192]{1,0:T(4,128)S(1)}, f32[4,8192]{1,0:T(4,128)S(1)}, u32[]{:S(2)}, u32[]{:S(2)}) collective-permute-start(f32[4,8192]{1,0:T(4,128)S(1)} %fusion.71), channel_id=1, source_target_pairs={{0,1},{1,2},{2,3},{3,4},{4,5},{5,6},{6,7},{7,8},{8,9},{9,10},{10,1... | collective-permute-start | bytes 393224 | tf_op jit(solution)/shard_map/while/body/eval_jaxpr/ppermute | solution.py:14
  174.6 7.9 %collective-permute-start.1 = (f32[4,8192]{1,0:T(4,128)S(1)}, f32[4,8192]{1,0:T(4,128)S(1)}, u32[]{:S(2)}, u32[]{:S(2)}) collective-permute-start(f32[4,8192]{1,0:T(4,128)S(1)} %fusion.71), channel_id=1, source_target_pairs={{0,1},{1,2},{2,3},{3,4},{4,5},{5,6},{6,7},{7,8},{8,9},{9,10},{10,1... | collective-permute-start | bytes 393224 | tf_op jit(solution)/shard_map/while/body/eval_jaxpr/ppermute | solution.py:14
  189.7 7.9 %collective-permute-start.1 = (f32[4,8192]{1,0:T(4,128)S(1)}, f32[4,8192]{1,0:T(4,128)S(1)}, u32[]{:S(2)}, u32[]{:S(2)}) collective-permute-start(f32[4,8192]{1,0:T(4,128)S(1)} %fusion.71), channel_id=1, source_target_pairs={{0,1},{1,2},{2,3},{3,4},{4,5},{5,6},{6,7},{7,8},{8,9},{9,10},{10,1... | collective-permute-start | bytes 393224 | tf_op jit(solution)/shard_map/while/body/eval_jaxpr/ppermute | solution.py:14
  204.7 7.9 %collective-permute-start.1 = (f32[4,8192]{1,0:T(4,128)S(1)}, f32[4,8192]{1,0:T(4,128)S(1)}, u32[]{:S(2)}, u32[]{:S(2)}) collective-permute-start(f32[4,8192]{1,0:T(4,128)S(1)} %fusion.71), channel_id=1, source_target_pairs={{0,1},{1,2},{2,3},{3,4},{4,5},{5,6},{6,7},{7,8},{8,9},{9,10},{10,1... | collective-permute-start | bytes 393224 | tf_op jit(solution)/shard_map/while/body/eval_jaxpr/ppermute | solution.py:14
  234.8 8.9 %collective-permute-start.1 = (f32[4,8192]{1,0:T(4,128)S(1)}, f32[4,8192]{1,0:T(4,128)S(1)}, u32[]{:S(2)}, u32[]{:S(2)}) collective-permute-start(f32[4,8192]{1,0:T(4,128)S(1)} %fusion.71), channel_id=1, source_target_pairs={{0,1},{1,2},{2,3},{3,4},{4,5},{5,6},{6,7},{7,8},{8,9},{9,10},{10,1... | collective-permute-start | bytes 393224 | tf_op jit(solution)/shard_map/while/body/eval_jaxpr/ppermute | solution.py:14
  234.9 8.8 %collective-permute-start = (bf16[4,8192]{1,0:T(4,128)(2,1)S(1)}, bf16[4,8192]{1,0:T(4,128)(2,1)S(1)}, u32[]{:S(2)}, u32[]{:S(2)}) collective-permute-start(bf16[4,8192]{1,0:T(4,128)(2,1)S(1)} %copy.160), channel_id=1, source_target_pairs={{0,1},{1,2},{2,3},{3,4},{4,5},{5,6},{6,7},{7,8},{8,9},{9,10},{10,1... | collective-permute-start | bytes 196616 | tf_op jit(solution)/shard_map/while/body/eval_jaxpr/ppermute | solution.py:14
  250.8 10.0 %collective-permute-start.1 = (f32[4,8192]{1,0:T(4,128)S(1)}, f32[4,8192]{1,0:T(4,128)S(1)}, u32[]{:S(2)}, u32[]{:S(2)}) collective-permute-start(f32[4,8192]{1,0:T(4,128)S(1)} %fusion.71), channel_id=1, source_target_pairs={{0,1},{1,2},{2,3},{3,4},{4,5},{5,6},{6,7},{7,8},{8,9},{9,10},{10,1... | collective-permute-start | bytes 393224 | tf_op jit(solution)/shard_map/while/body/eval_jaxpr/ppermute | solution.py:14
  250.9 9.9 %collective-permute-start = (bf16[4,8192]{1,0:T(4,128)(2,1)S(1)}, bf16[4,8192]{1,0:T(4,128)(2,1)S(1)}, u32[]{:S(2)}, u32[]{:S(2)}) collective-permute-start(bf16[4,8192]{1,0:T(4,128)(2,1)S(1)} %copy.160), channel_id=1, source_target_pairs={{0,1},{1,2},{2,3},{3,4},{4,5},{5,6},{6,7},{7,8},{8,9},{9,10},{10,1... | collective-permute-start | bytes 196616 | tf_op jit(solution)/shard_map/while/body/eval_jaxpr/ppermute | solution.py:14
  251.2 9.6 %collective-permute-start.2 = (f32[4,64]{1,0:T(4,128)S(1)}, f32[4,64]{1,0:T(4,128)S(1)}, u32[]{:S(2)}, u32[]{:S(2)}) collective-permute-start(f32[4,64]{1,0:T(4,128)S(1)} %get-tuple-element.508), channel_id=1, source_target_pairs={{0,1},{1,2},{2,3},{3,4},{4,5},{5,6},{6,7},{7,8},{8,9},{9,10},{10,1... | collective-permute-start | bytes 3080 | tf_op jit(solution)/shard_map/while/body/eval_jaxpr/ppermute | solution.py:14
  251.3 9.6 %collective-permute-start.3 = (f32[4,64]{1,0:T(4,128)S(1)}, f32[4,64]{1,0:T(4,128)S(1)}, u32[]{:S(2)}, u32[]{:S(2)}) collective-permute-start(f32[4,64]{1,0:T(4,128)S(1)} %get-tuple-element.509), channel_id=1, source_target_pairs={{0,1},{1,2},{2,3},{3,4},{4,5},{5,6},{6,7},{7,8},{8,9},{9,10},{10,1... | collective-permute-start | bytes 3080 | tf_op jit(solution)/shard_map/while/body/eval_jaxpr/ppermute | solution.py:14
  268.0 9.2 %collective-permute-start.1 = (f32[4,8192]{1,0:T(4,128)S(1)}, f32[4,8192]{1,0:T(4,128)S(1)}, u32[]{:S(2)}, u32[]{:S(2)}) collective-permute-start(f32[4,8192]{1,0:T(4,128)S(1)} %fusion.71), channel_id=1, source_target_pairs={{0,1},{1,2},{2,3},{3,4},{4,5},{5,6},{6,7},{7,8},{8,9},{9,10},{10,1... | collective-permute-start | bytes 393224 | tf_op jit(solution)/shard_map/while/body/eval_jaxpr/ppermute | solution.py:14
  268.1 9.1 %collective-permute-start = (bf16[4,8192]{1,0:T(4,128)(2,1)S(1)}, bf16[4,8192]{1,0:T(4,128)(2,1)S(1)}, u32[]{:S(2)}, u32[]{:S(2)}) collective-permute-start(bf16[4,8192]{1,0:T(4,128)(2,1)S(1)} %copy.160), channel_id=1, source_target_pairs={{0,1},{1,2},{2,3},{3,4},{4,5},{5,6},{6,7},{7,8},{8,9},{9,10},{10,1... | collective-permute-start | bytes 196616 | tf_op jit(solution)/shard_map/while/body/eval_jaxpr/ppermute | solution.py:14
  268.1 9.0 %collective-permute-start.2 = (f32[4,64]{1,0:T(4,128)S(1)}, f32[4,64]{1,0:T(4,128)S(1)}, u32[]{:S(2)}, u32[]{:S(2)}) collective-permute-start(f32[4,64]{1,0:T(4,128)S(1)} %get-tuple-element.508), channel_id=1, source_target_pairs={{0,1},{1,2},{2,3},{3,4},{4,5},{5,6},{6,7},{7,8},{8,9},{9,10},{10,1... | collective-permute-start | bytes 3080 | tf_op jit(solution)/shard_map/while/body/eval_jaxpr/ppermute | solution.py:14
  268.2 9.0 %collective-permute-start.3 = (f32[4,64]{1,0:T(4,128)S(1)}, f32[4,64]{1,0:T(4,128)S(1)}, u32[]{:S(2)}, u32[]{:S(2)}) collective-permute-start(f32[4,64]{1,0:T(4,128)S(1)} %get-tuple-element.509), channel_id=1, source_target_pairs={{0,1},{1,2},{2,3},{3,4},{4,5},{5,6},{6,7},{7,8},{8,9},{9,10},{10,1... | collective-permute-start | bytes 3080 | tf_op jit(solution)/shard_map/while/body/eval_jaxpr/ppermute | solution.py:14
  284.3 8.4 %collective-permute-start.1 = (f32[4,8192]{1,0:T(4,128)S(1)}, f32[4,8192]{1,0:T(4,128)S(1)}, u32[]{:S(2)}, u32[]{:S(2)}) collective-permute-start(f32[4,8192]{1,0:T(4,128)S(1)} %fusion.71), channel_id=1, source_target_pairs={{0,1},{1,2},{2,3},{3,4},{4,5},{5,6},{6,7},{7,8},{8,9},{9,10},{10,1... | collective-permute-start | bytes 393224 | tf_op jit(solution)/shard_map/while/body/eval_jaxpr/ppermute | solution.py:14
  284.4 8.3 %collective-permute-start = (bf16[4,8192]{1,0:T(4,128)(2,1)S(1)}, bf16[4,8192]{1,0:T(4,128)(2,1)S(1)}, u32[]{:S(2)}, u32[]{:S(2)}) collective-permute-start(bf16[4,8192]{1,0:T(4,128)(2,1)S(1)} %copy.160), channel_id=1, source_target_pairs={{0,1},{1,2},{2,3},{3,4},{4,5},{5,6},{6,7},{7,8},{8,9},{9,10},{10,1... | collective-permute-start | bytes 196616 | tf_op jit(solution)/shard_map/while/body/eval_jaxpr/ppermute | solution.py:14
  284.5 8.2 %collective-permute-start.2 = (f32[4,64]{1,0:T(4,128)S(1)}, f32[4,64]{1,0:T(4,128)S(1)}, u32[]{:S(2)}, u32[]{:S(2)}) collective-permute-start(f32[4,64]{1,0:T(4,128)S(1)} %get-tuple-element.508), channel_id=1, source_target_pairs={{0,1},{1,2},{2,3},{3,4},{4,5},{5,6},{6,7},{7,8},{8,9},{9,10},{10,1... | collective-permute-start | bytes 3080 | tf_op jit(solution)/shard_map/while/body/eval_jaxpr/ppermute | solution.py:14
  284.6 8.1 %collective-permute-start.3 = (f32[4,64]{1,0:T(4,128)S(1)}, f32[4,64]{1,0:T(4,128)S(1)}, u32[]{:S(2)}, u32[]{:S(2)}) collective-permute-start(f32[4,64]{1,0:T(4,128)S(1)} %get-tuple-element.509), channel_id=1, source_target_pairs={{0,1},{1,2},{2,3},{3,4},{4,5},{5,6},{6,7},{7,8},{8,9},{9,10},{10,1... | collective-permute-start | bytes 3080 | tf_op jit(solution)/shard_map/while/body/eval_jaxpr/ppermute | solution.py:14
  (57 other events, 317.1 us)
where the time goes:
time: 326 us; the launch traced here: 324 us
  waiting for transfers between devices  82.5 us (25%)
  blocking collectives  66.1 us (20%)
  matrix products  53.6 us (16%)
  starting transfers between devices  50.2 us (15%)
  local copies, waits for them, and re-layouts  29.6 us (9%)
  other arithmetic  29.3 us (9%)
  loops' own time  12.3 us (4%)
    ppermute x64, waiting for transfers between devices, from_behind(): lax.ppermute(x, axis, [(i, (i + by) % devices) for i in range(devices)])  82.5 us
    ppermute x64, starting transfers between devices, from_behind(): lax.ppermute(x, axis, [(i, (i + by) % devices) for i in range(devices)])  50.2 us
    dot_general x17, matrix products, attend(): jnp.einsum('rkgd,nkd->rkgn', grouped, keys_grouped, preferred_element_typ...  40.8 us
    all_gather x1, blocking collectives, local(): keys_piece = lax.all_gather(new_keys, 'ctx', axis=0, tiled=True)  35.9 us
    all_gather x1, blocking collectives, local(): values_piece = lax.all_gather(new_values, 'ctx', axis=0, tiled=True)  30.2 us
    while x80, local copies, waits for them, and re-layouts  19 us
    dot_general x17, matrix products, attend(): jnp.einsum('rkgn,nkd->rkgd', weights.astype(jnp.bfloat16), values_grouped...  12.8 us
    another operation x1, loops' own time, local(): lax.fori_loop(0, count, hop_one, (queries,) + empty_state(rows, heads))  12.3 us
  transfers between devices with their start and end apart: 64, of which 17 were waited for; matrix products, arithmetic and copies ran while one was open for 0% of the time, Pallas kernels for 0%

commit v1 on v0

--- a/solution.py
+++ b/solution.py
@@ -86,8 +86,11 @@
     def attend_cache(held, positions):
         return attend(held, positions, cache_keys, cache_values, cache_pos, cache_live)
 
-    keys_piece = lax.all_gather(new_keys, "ctx", axis=0, tiled=True)
-    values_piece = lax.all_gather(new_values, "ctx", axis=0, tiled=True)
+    keys_piece, values_piece = jnp.split(
+        lax.all_gather(jnp.concatenate([new_keys, new_values], axis=1), "ctx", axis=0, tiled=True),
+        [new_keys.shape[1]],
+        axis=1,
+    )
     piece_rows = keys_piece.shape[0]
     key_pos = length + lax.iota(jnp.int32, piece_rows)
     span_state = combine(

time: 326 us -> 269 us (0.83)
  blocking collectives: 66.1 us -> 36 us
  matrix products: 53.6 us -> 27.9 us
  waiting for transfers between devices: 82.5 us -> 72.5 us
  starting transfers between devices: 50.2 us -> 58.3 us
    all_gather x2 -> x1, blocking collectives: 66.1 us -> 36 us  [local(): lax.all_gather(jnp.concatenate([new_keys, new_values], axis=1), 'ctx', ax...]
    dot_general x17, matrix products: 40.8 us -> 15.4 us  [attend(): jnp.einsum('rkgd,nkd->rkgn', grouped, keys_grouped, preferred_element_typ...]
    ppermute x64, waiting for transfers between devices: 82.5 us -> 72.5 us  [from_behind(): lax.ppermute(x, axis, [(i, (i + by) % devices) for i in range(devices)])]
    ppermute x64, starting transfers between devices: 50.2 us -> 58.3 us  [from_behind(): lax.ppermute(x, axis, [(i, (i + by) % devices) for i in range(devices)])]
  transfers between devices with their start and end apart: 64 -> 64, of which waited for: 17 -> 16; matrix products, arithmetic and copies ran while one was open for 0% -> 0% of each run, Pallas kernels for 0% -> 0%
where the time goes in v1:
time: 269 us; the launch traced here: 267 us
  waiting for transfers between devices  72.5 us (27%)
  starting transfers between devices  58.3 us (22%)
  blocking collectives  36 us (13%)
  other arithmetic  30 us (11%)
  local copies, waits for them, and re-layouts  29.8 us (11%)
  matrix products  27.9 us (10%)
  loops' own time  12.2 us (5%)
    ppermute x64, waiting for transfers between devices, from_behind(): lax.ppermute(x, axis, [(i, (i + by) % devices) for i in range(devices)])  72.5 us
    ppermute x64, starting transfers between devices, from_behind(): lax.ppermute(x, axis, [(i, (i + by) % devices) for i in range(devices)])  58.3 us
    all_gather x1, blocking collectives, local(): lax.all_gather(jnp.concatenate([new_keys, new_values], axis=1), 'ctx', ax...  36 us
    while x80, local copies, waits for them, and re-layouts  19 us
    dot_general x17, matrix products, attend(): jnp.einsum('rkgd,nkd->rkgn', grouped, keys_grouped, preferred_element_typ...  15.4 us
    dot_general x17, matrix products, attend(): jnp.einsum('rkgn,nkd->rkgd', weights.astype(jnp.bfloat16), values_grouped...  12.6 us
    another operation x1, loops' own time, local(): lax.fori_loop(0, count, hop_one, (queries,) + empty_state(rows, heads))  12.2 us
    lt x16, other arithmetic, local(): cache_live = cache_pos < length  11.5 us
  transfers between devices with their start and end apart: 64, of which 16 were waited for; matrix products, arithmetic and copies ran while one was open for 0% of the time, Pallas kernels for 0%

profile of v1, /device:TPU:2, one launch (start us, length us, event | category | flops | bytes accessed | tf_op | source)
XLA Modules:
  0.0 267.4 jit_solution(12737388205350132350)
XLA Ops:
  3.3 36.0 %all-gather = bf16[16,4,1024]{2,1,0:T(4,128)(2,1)S(1)} all-gather(bf16[1,4,1024]{2,1,0:T(4,128)(2,1)S(1)} %maximum_bitcast_fusion), channel_id=1, replica_groups=mesh['req'=16,'ctx'=16] {'ctx'}, dimensions={0}, use_global_device_ids=true | all-gather | bytes 139264 | tf_op jit(solution)/shard_map/all_gather | solution.py:90
  42.4 4.1 %reshape.245 = bf16[2048,4,128]{2,1,0:T(4,128)(2,1)} reshape(bf16[2048,512]{1,0:T(8,128)(2,1)} %param.13) | data formatting | bytes 4194304 | tf_op jit(solution)/shard_map/while/body/eval_jaxpr/reshape | solution.py:23
  46.6 219.4 %while.24 = (s32[]{:T(128)}, bf16[4,8192]{1,0:T(4,128)(2,1)S(1)}, f32[4,8192]{1,0:T(4,128)S(1)}, f32[4,64]{1,0:T(4,128)S(1)}, f32[4,64]{1,0:T(4,128)S(1)}, /*ind...) while((s32[]{:T(128)}, bf16[4,8192]{1,0:T(4,128)(2,1)S(1)}, ...), condition=%wide.wide.region_4.5_spmd.clone.clone, body=%wide.wide.region_1.4_spmd.clone.clone.sunk | while | flops 273275904 | bytes 21383824 | solution.py:108
  53.3 6.7 %collective-permute-done.2 = f32[4,64]{1,0:T(4,128)S(1)} collective-permute-done((f32[4,64]{1,0:T(4,128)S(1)}, f32[4,64]{1,0:T(4,128)S(1)}, u32[]{:S(2)}, u32[]{:S(2)}) %collective-permute-start.2) | collective-permute-done | bytes 1056 | tf_op jit(solution)/shard_map/while/body/eval_jaxpr/ppermute | solution.py:14
  65.8 3.5 %collective-permute-start.3 = (f32[4,64]{1,0:T(4,128)S(1)}, f32[4,64]{1,0:T(4,128)S(1)}, u32[]{:S(2)}, u32[]{:S(2)}) collective-permute-start(f32[4,64]{1,0:T(4,128)S(1)} %get-tuple-element.511), channel_id=1, source_target_pairs={{0,1},{1,2},{2,3},{3,4},{4,5},{5,6},{6,7},{7,8},{8,9},{9,10},{10,1... | collective-permute-start | bytes 3080 | tf_op jit(solution)/shard_map/while/body/eval_jaxpr/ppermute | solution.py:14
  69.3 4.1 %collective-permute-done.2 = f32[4,64]{1,0:T(4,128)S(1)} collective-permute-done((f32[4,64]{1,0:T(4,128)S(1)}, f32[4,64]{1,0:T(4,128)S(1)}, u32[]{:S(2)}, u32[]{:S(2)}) %collective-permute-start.2) | collective-permute-done | bytes 1056 | tf_op jit(solution)/shard_map/while/body/eval_jaxpr/ppermute | solution.py:14
  83.4 3.8 %collective-permute-done.2 = f32[4,64]{1,0:T(4,128)S(1)} collective-permute-done((f32[4,64]{1,0:T(4,128)S(1)}, f32[4,64]{1,0:T(4,128)S(1)}, u32[]{:S(2)}, u32[]{:S(2)}) %collective-permute-start.2) | collective-permute-done | bytes 1056 | tf_op jit(solution)/shard_map/while/body/eval_jaxpr/ppermute | solution.py:14
  94.4 3.2 %collective-permute-start.3 = (f32[4,64]{1,0:T(4,128)S(1)}, f32[4,64]{1,0:T(4,128)S(1)}, u32[]{:S(2)}, u32[]{:S(2)}) collective-permute-start(f32[4,64]{1,0:T(4,128)S(1)} %get-tuple-element.511), channel_id=1, source_target_pairs={{0,1},{1,2},{2,3},{3,4},{4,5},{5,6},{6,7},{7,8},{8,9},{9,10},{10,1... | collective-permute-start | bytes 3080 | tf_op jit(solution)/shard_map/while/body/eval_jaxpr/ppermute | solution.py:14
  97.5 4.6 %collective-permute-done.2 = f32[4,64]{1,0:T(4,128)S(1)} collective-permute-done((f32[4,64]{1,0:T(4,128)S(1)}, f32[4,64]{1,0:T(4,128)S(1)}, u32[]{:S(2)}, u32[]{:S(2)}) %collective-permute-start.2) | collective-permute-done | bytes 1056 | tf_op jit(solution)/shard_map/while/body/eval_jaxpr/ppermute | solution.py:14
  108.0 3.7 %collective-permute-start.3 = (f32[4,64]{1,0:T(4,128)S(1)}, f32[4,64]{1,0:T(4,128)S(1)}, u32[]{:S(2)}, u32[]{:S(2)}) collective-permute-start(f32[4,64]{1,0:T(4,128)S(1)} %get-tuple-element.511), channel_id=1, source_target_pairs={{0,1},{1,2},{2,3},{3,4},{4,5},{5,6},{6,7},{7,8},{8,9},{9,10},{10,1... | collective-permute-start | bytes 3080 | tf_op jit(solution)/shard_map/while/body/eval_jaxpr/ppermute | solution.py:14
  111.6 5.6 %collective-permute-done.2 = f32[4,64]{1,0:T(4,128)S(1)} collective-permute-done((f32[4,64]{1,0:T(4,128)S(1)}, f32[4,64]{1,0:T(4,128)S(1)}, u32[]{:S(2)}, u32[]{:S(2)}) %collective-permute-start.2) | collective-permute-done | bytes 1056 | tf_op jit(solution)/shard_map/while/body/eval_jaxpr/ppermute | solution.py:14
  125.0 6.5 %collective-permute-done.2 = f32[4,64]{1,0:T(4,128)S(1)} collective-permute-done((f32[4,64]{1,0:T(4,128)S(1)}, f32[4,64]{1,0:T(4,128)S(1)}, u32[]{:S(2)}, u32[]{:S(2)}) %collective-permute-start.2) | collective-permute-done | bytes 1056 | tf_op jit(solution)/shard_map/while/body/eval_jaxpr/ppermute | solution.py:14
  137.3 2.7 %collective-permute-start.3 = (f32[4,64]{1,0:T(4,128)S(1)}, f32[4,64]{1,0:T(4,128)S(1)}, u32[]{:S(2)}, u32[]{:S(2)}) collective-permute-start(f32[4,64]{1,0:T(4,128)S(1)} %get-tuple-element.511), channel_id=1, source_target_pairs={{0,1},{1,2},{2,3},{3,4},{4,5},{5,6},{6,7},{7,8},{8,9},{9,10},{10,1... | collective-permute-start | bytes 3080 | tf_op jit(solution)/shard_map/while/body/eval_jaxpr/ppermute | solution.py:14
  140.0 4.9 %collective-permute-done.2 = f32[4,64]{1,0:T(4,128)S(1)} collective-permute-done((f32[4,64]{1,0:T(4,128)S(1)}, f32[4,64]{1,0:T(4,128)S(1)}, u32[]{:S(2)}, u32[]{:S(2)}) %collective-permute-start.2) | collective-permute-done | bytes 1056 | tf_op jit(solution)/shard_map/while/body/eval_jaxpr/ppermute | solution.py:14
  151.6 2.7 collective-permute-start.3
  154.3 4.1 %collective-permute-done.2 = f32[4,64]{1,0:T(4,128)S(1)} collective-permute-done((f32[4,64]{1,0:T(4,128)S(1)}, f32[4,64]{1,0:T(4,128)S(1)}, u32[]{:S(2)}, u32[]{:S(2)}) %collective-permute-start.2) | collective-permute-done | bytes 1056 | tf_op jit(solution)/shard_map/while/body/eval_jaxpr/ppermute | solution.py:14
  167.7 4.1 %collective-permute-done.2 = f32[4,64]{1,0:T(4,128)S(1)} collective-permute-done((f32[4,64]{1,0:T(4,128)S(1)}, f32[4,64]{1,0:T(4,128)S(1)}, u32[]{:S(2)}, u32[]{:S(2)}) %collective-permute-start.2) | collective-permute-done | bytes 1056 | tf_op jit(solution)/shard_map/while/body/eval_jaxpr/ppermute | solution.py:14
  181.1 4.1 %collective-permute-done.2 = f32[4,64]{1,0:T(4,128)S(1)} collective-permute-done((f32[4,64]{1,0:T(4,128)S(1)}, f32[4,64]{1,0:T(4,128)S(1)}, u32[]{:S(2)}, u32[]{:S(2)}) %collective-permute-start.2) | collective-permute-done | bytes 1056 | tf_op jit(solution)/shard_map/while/body/eval_jaxpr/ppermute | solution.py:14
  194.6 4.1 %collective-permute-done.2 = f32[4,64]{1,0:T(4,128)S(1)} collective-permute-done((f32[4,64]{1,0:T(4,128)S(1)}, f32[4,64]{1,0:T(4,128)S(1)}, u32[]{:S(2)}, u32[]{:S(2)}) %collective-permute-start.2) | collective-permute-done | bytes 1056 | tf_op jit(solution)/shard_map/while/body/eval_jaxpr/ppermute | solution.py:14
  208.0 4.1 %collective-permute-done.2 = f32[4,64]{1,0:T(4,128)S(1)} collective-permute-done((f32[4,64]{1,0:T(4,128)S(1)}, f32[4,64]{1,0:T(4,128)S(1)}, u32[]{:S(2)}, u32[]{:S(2)}) %collective-permute-start.2) | collective-permute-done | bytes 1056 | tf_op jit(solution)/shard_map/while/body/eval_jaxpr/ppermute | solution.py:14
  221.5 4.1 %collective-permute-done.2 = f32[4,64]{1,0:T(4,128)S(1)} collective-permute-done((f32[4,64]{1,0:T(4,128)S(1)}, f32[4,64]{1,0:T(4,128)S(1)}, u32[]{:S(2)}, u32[]{:S(2)}) %collective-permute-start.2) | collective-permute-done | bytes 1056 | tf_op jit(solution)/shard_map/while/body/eval_jaxpr/ppermute | solution.py:14
  235.3 3.8 %collective-permute-done.2 = f32[4,64]{1,0:T(4,128)S(1)} collective-permute-done((f32[4,64]{1,0:T(4,128)S(1)}, f32[4,64]{1,0:T(4,128)S(1)}, u32[]{:S(2)}, u32[]{:S(2)}) %collective-permute-start.2) | collective-permute-done | bytes 1056 | tf_op jit(solution)/shard_map/while/body/eval_jaxpr/ppermute | solution.py:14
  249.0 3.5 %collective-permute-done.2 = f32[4,64]{1,0:T(4,128)S(1)} collective-permute-done((f32[4,64]{1,0:T(4,128)S(1)}, f32[4,64]{1,0:T(4,128)S(1)}, u32[]{:S(2)}, u32[]{:S(2)}) %collective-permute-start.2) | collective-permute-done | bytes 1056 | tf_op jit(solution)/shard_map/while/body/eval_jaxpr/ppermute | solution.py:14
  261.9 4.1 %collective-permute-done.2 = f32[4,64]{1,0:T(4,128)S(1)} collective-permute-done((f32[4,64]{1,0:T(4,128)S(1)}, f32[4,64]{1,0:T(4,128)S(1)}, u32[]{:S(2)}, u32[]{:S(2)}) %collective-permute-start.2) | collective-permute-done | bytes 1056 | tf_op jit(solution)/shard_map/while/body/eval_jaxpr/ppermute | solution.py:14
  (445 shorter events, 126.6 us)
Async XLA Ops:
  52.1 7.9 %collective-permute-start.1 = (f32[4,8192]{1,0:T(4,128)S(1)}, f32[4,8192]{1,0:T(4,128)S(1)}, u32[]{:S(2)}, u32[]{:S(2)}) collective-permute-start(f32[4,8192]{1,0:T(4,128)S(1)} %fusion.72), channel_id=1, source_target_pairs={{0,1},{1,2},{2,3},{3,4},{4,5},{5,6},{6,7},{7,8},{8,9},{9,10},{10,1... | collective-permute-start | bytes 393224 | tf_op jit(solution)/shard_map/while/body/eval_jaxpr/ppermute | solution.py:14
  65.5 7.9 %collective-permute-start.1 = (f32[4,8192]{1,0:T(4,128)S(1)}, f32[4,8192]{1,0:T(4,128)S(1)}, u32[]{:S(2)}, u32[]{:S(2)}) collective-permute-start(f32[4,8192]{1,0:T(4,128)S(1)} %fusion.72), channel_id=1, source_target_pairs={{0,1},{1,2},{2,3},{3,4},{4,5},{5,6},{6,7},{7,8},{8,9},{9,10},{10,1... | collective-permute-start | bytes 393224 | tf_op jit(solution)/shard_map/while/body/eval_jaxpr/ppermute | solution.py:14
  79.0 8.3 %collective-permute-start.1 = (f32[4,8192]{1,0:T(4,128)S(1)}, f32[4,8192]{1,0:T(4,128)S(1)}, u32[]{:S(2)}, u32[]{:S(2)}) collective-permute-start(f32[4,8192]{1,0:T(4,128)S(1)} %fusion.72), channel_id=1, source_target_pairs={{0,1},{1,2},{2,3},{3,4},{4,5},{5,6},{6,7},{7,8},{8,9},{9,10},{10,1... | collective-permute-start | bytes 393224 | tf_op jit(solution)/shard_map/while/body/eval_jaxpr/ppermute | solution.py:14
  79.1 8.2 %collective-permute-start = (bf16[4,8192]{1,0:T(4,128)(2,1)S(1)}, bf16[4,8192]{1,0:T(4,128)(2,1)S(1)}, u32[]{:S(2)}, u32[]{:S(2)}) collective-permute-start(bf16[4,8192]{1,0:T(4,128)(2,1)S(1)} %copy.160), channel_id=1, source_target_pairs={{0,1},{1,2},{2,3},{3,4},{4,5},{5,6},{6,7},{7,8},{8,9},{9,10},{10,1... | collective-permute-start | bytes 196616 | tf_op jit(solution)/shard_map/while/body/eval_jaxpr/ppermute | solution.py:14
  92.8 9.4 %collective-permute-start.1 = (f32[4,8192]{1,0:T(4,128)S(1)}, f32[4,8192]{1,0:T(4,128)S(1)}, u32[]{:S(2)}, u32[]{:S(2)}) collective-permute-start(f32[4,8192]{1,0:T(4,128)S(1)} %fusion.72), channel_id=1, source_target_pairs={{0,1},{1,2},{2,3},{3,4},{4,5},{5,6},{6,7},{7,8},{8,9},{9,10},{10,1... | collective-permute-start | bytes 393224 | tf_op jit(solution)/shard_map/while/body/eval_jaxpr/ppermute | solution.py:14
  92.9 9.3 %collective-permute-start = (bf16[4,8192]{1,0:T(4,128)(2,1)S(1)}, bf16[4,8192]{1,0:T(4,128)(2,1)S(1)}, u32[]{:S(2)}, u32[]{:S(2)}) collective-permute-start(bf16[4,8192]{1,0:T(4,128)(2,1)S(1)} %copy.160), channel_id=1, source_target_pairs={{0,1},{1,2},{2,3},{3,4},{4,5},{5,6},{6,7},{7,8},{8,9},{9,10},{10,1... | collective-permute-start | bytes 196616 | tf_op jit(solution)/shard_map/while/body/eval_jaxpr/ppermute | solution.py:14
  107.7 9.6 %collective-permute-start.1 = (f32[4,8192]{1,0:T(4,128)S(1)}, f32[4,8192]{1,0:T(4,128)S(1)}, u32[]{:S(2)}, u32[]{:S(2)}) collective-permute-start(f32[4,8192]{1,0:T(4,128)S(1)} %fusion.72), channel_id=1, source_target_pairs={{0,1},{1,2},{2,3},{3,4},{4,5},{5,6},{6,7},{7,8},{8,9},{9,10},{10,1... | collective-permute-start | bytes 393224 | tf_op jit(solution)/shard_map/while/body/eval_jaxpr/ppermute | solution.py:14
  107.8 9.5 %collective-permute-start = (bf16[4,8192]{1,0:T(4,128)(2,1)S(1)}, bf16[4,8192]{1,0:T(4,128)(2,1)S(1)}, u32[]{:S(2)}, u32[]{:S(2)}) collective-permute-start(bf16[4,8192]{1,0:T(4,128)(2,1)S(1)} %copy.160), channel_id=1, source_target_pairs={{0,1},{1,2},{2,3},{3,4},{4,5},{5,6},{6,7},{7,8},{8,9},{9,10},{10,1... | collective-permute-start | bytes 196616 | tf_op jit(solution)/shard_map/while/body/eval_jaxpr/ppermute | solution.py:14
  107.9 9.3 %collective-permute-start.2 = (f32[4,64]{1,0:T(4,128)S(1)}, f32[4,64]{1,0:T(4,128)S(1)}, u32[]{:S(2)}, u32[]{:S(2)}) collective-permute-start(f32[4,64]{1,0:T(4,128)S(1)} %get-tuple-element.510), channel_id=1, source_target_pairs={{0,1},{1,2},{2,3},{3,4},{4,5},{5,6},{6,7},{7,8},{8,9},{9,10},{10,1... | collective-permute-start | bytes 3080 | tf_op jit(solution)/shard_map/while/body/eval_jaxpr/ppermute | solution.py:14
  108.0 9.3 %collective-permute-start.3 = (f32[4,64]{1,0:T(4,128)S(1)}, f32[4,64]{1,0:T(4,128)S(1)}, u32[]{:S(2)}, u32[]{:S(2)}) collective-permute-start(f32[4,64]{1,0:T(4,128)S(1)} %get-tuple-element.511), channel_id=1, source_target_pairs={{0,1},{1,2},{2,3},{3,4},{4,5},{5,6},{6,7},{7,8},{8,9},{9,10},{10,1... | collective-permute-start | bytes 3080 | tf_op jit(solution)/shard_map/while/body/eval_jaxpr/ppermute | solution.py:14
  122.8 8.7 %collective-permute-start.1 = (f32[4,8192]{1,0:T(4,128)S(1)}, f32[4,8192]{1,0:T(4,128)S(1)}, u32[]{:S(2)}, u32[]{:S(2)}) collective-permute-start(f32[4,8192]{1,0:T(4,128)S(1)} %fusion.72), channel_id=1, source_target_pairs={{0,1},{1,2},{2,3},{3,4},{4,5},{5,6},{6,7},{7,8},{8,9},{9,10},{10,1... | collective-permute-start | bytes 393224 | tf_op jit(solution)/shard_map/while/body/eval_jaxpr/ppermute | solution.py:14
  122.9 8.6 %collective-permute-start = (bf16[4,8192]{1,0:T(4,128)(2,1)S(1)}, bf16[4,8192]{1,0:T(4,128)(2,1)S(1)}, u32[]{:S(2)}, u32[]{:S(2)}) collective-permute-start(bf16[4,8192]{1,0:T(4,128)(2,1)S(1)} %copy.160), channel_id=1, source_target_pairs={{0,1},{1,2},{2,3},{3,4},{4,5},{5,6},{6,7},{7,8},{8,9},{9,10},{10,1... | collective-permute-start | bytes 196616 | tf_op jit(solution)/shard_map/while/body/eval_jaxpr/ppermute | solution.py:14
  123.0 8.5 %collective-permute-start.2 = (f32[4,64]{1,0:T(4,128)S(1)}, f32[4,64]{1,0:T(4,128)S(1)}, u32[]{:S(2)}, u32[]{:S(2)}) collective-permute-start(f32[4,64]{1,0:T(4,128)S(1)} %get-tuple-element.510), channel_id=1, source_target_pairs={{0,1},{1,2},{2,3},{3,4},{4,5},{5,6},{6,7},{7,8},{8,9},{9,10},{10,1... | collective-permute-start | bytes 3080 | tf_op jit(solution)/shard_map/while/body/eval_jaxpr/ppermute | solution.py:14
  123.1 8.4 %collective-permute-start.3 = (f32[4,64]{1,0:T(4,128)S(1)}, f32[4,64]{1,0:T(4,128)S(1)}, u32[]{:S(2)}, u32[]{:S(2)}) collective-permute-start(f32[4,64]{1,0:T(4,128)S(1)} %get-tuple-element.511), channel_id=1, source_target_pairs={{0,1},{1,2},{2,3},{3,4},{4,5},{5,6},{6,7},{7,8},{8,9},{9,10},{10,1... | collective-permute-start | bytes 3080 | tf_op jit(solution)/shard_map/while/body/eval_jaxpr/ppermute | solution.py:14
  137.0 7.9 %collective-permute-start.1 = (f32[4,8192]{1,0:T(4,128)S(1)}, f32[4,8192]{1,0:T(4,128)S(1)}, u32[]{:S(2)}, u32[]{:S(2)}) collective-permute-start(f32[4,8192]{1,0:T(4,128)S(1)} %fusion.72), channel_id=1, source_target_pairs={{0,1},{1,2},{2,3},{3,4},{4,5},{5,6},{6,7},{7,8},{8,9},{9,10},{10,1... | collective-permute-start | bytes 393224 | tf_op jit(solution)/shard_map/while/body/eval_jaxpr/ppermute | solution.py:14
  150.5 7.9 %collective-permute-start.1 = (f32[4,8192]{1,0:T(4,128)S(1)}, f32[4,8192]{1,0:T(4,128)S(1)}, u32[]{:S(2)}, u32[]{:S(2)}) collective-permute-start(f32[4,8192]{1,0:T(4,128)S(1)} %fusion.72), channel_id=1, source_target_pairs={{0,1},{1,2},{2,3},{3,4},{4,5},{5,6},{6,7},{7,8},{8,9},{9,10},{10,1... | collective-permute-start | bytes 393224 | tf_op jit(solution)/shard_map/while/body/eval_jaxpr/ppermute | solution.py:14
  163.9 7.9 %collective-permute-start.1 = (f32[4,8192]{1,0:T(4,128)S(1)}, f32[4,8192]{1,0:T(4,128)S(1)}, u32[]{:S(2)}, u32[]{:S(2)}) collective-permute-start(f32[4,8192]{1,0:T(4,128)S(1)} %fusion.72), channel_id=1, source_target_pairs={{0,1},{1,2},{2,3},{3,4},{4,5},{5,6},{6,7},{7,8},{8,9},{9,10},{10,1... | collective-permute-start | bytes 393224 | tf_op jit(solution)/shard_map/while/body/eval_jaxpr/ppermute | solution.py:14
  177.3 7.9 %collective-permute-start.1 = (f32[4,8192]{1,0:T(4,128)S(1)}, f32[4,8192]{1,0:T(4,128)S(1)}, u32[]{:S(2)}, u32[]{:S(2)}) collective-permute-start(f32[4,8192]{1,0:T(4,128)S(1)} %fusion.72), channel_id=1, source_target_pairs={{0,1},{1,2},{2,3},{3,4},{4,5},{5,6},{6,7},{7,8},{8,9},{9,10},{10,1... | collective-permute-start | bytes 393224 | tf_op jit(solution)/shard_map/while/body/eval_jaxpr/ppermute | solution.py:14
  190.8 7.9 %collective-permute-start.1 = (f32[4,8192]{1,0:T(4,128)S(1)}, f32[4,8192]{1,0:T(4,128)S(1)}, u32[]{:S(2)}, u32[]{:S(2)}) collective-permute-start(f32[4,8192]{1,0:T(4,128)S(1)} %fusion.72), channel_id=1, source_target_pairs={{0,1},{1,2},{2,3},{3,4},{4,5},{5,6},{6,7},{7,8},{8,9},{9,10},{10,1... | collective-permute-start | bytes 393224 | tf_op jit(solution)/shard_map/while/body/eval_jaxpr/ppermute | solution.py:14
  204.2 7.9 %collective-permute-start.1 = (f32[4,8192]{1,0:T(4,128)S(1)}, f32[4,8192]{1,0:T(4,128)S(1)}, u32[]{:S(2)}, u32[]{:S(2)}) collective-permute-start(f32[4,8192]{1,0:T(4,128)S(1)} %fusion.72), channel_id=1, source_target_pairs={{0,1},{1,2},{2,3},{3,4},{4,5},{5,6},{6,7},{7,8},{8,9},{9,10},{10,1... | collective-permute-start | bytes 393224 | tf_op jit(solution)/shard_map/while/body/eval_jaxpr/ppermute | solution.py:14
  217.6 7.9 %collective-permute-start.1 = (f32[4,8192]{1,0:T(4,128)S(1)}, f32[4,8192]{1,0:T(4,128)S(1)}, u32[]{:S(2)}, u32[]{:S(2)}) collective-permute-start(f32[4,8192]{1,0:T(4,128)S(1)} %fusion.72), channel_id=1, source_target_pairs={{0,1},{1,2},{2,3},{3,4},{4,5},{5,6},{6,7},{7,8},{8,9},{9,10},{10,1... | collective-permute-start | bytes 393224 | tf_op jit(solution)/shard_map/while/body/eval_jaxpr/ppermute | solution.py:14
  231.1 8.1 %collective-permute-start.1 = (f32[4,8192]{1,0:T(4,128)S(1)}, f32[4,8192]{1,0:T(4,128)S(1)}, u32[]{:S(2)}, u32[]{:S(2)}) collective-permute-start(f32[4,8192]{1,0:T(4,128)S(1)} %fusion.72), channel_id=1, source_target_pairs={{0,1},{1,2},{2,3},{3,4},{4,5},{5,6},{6,7},{7,8},{8,9},{9,10},{10,1... | collective-permute-start | bytes 393224 | tf_op jit(solution)/shard_map/while/body/eval_jaxpr/ppermute | solution.py:14
  231.2 8.0 %collective-permute-start = (bf16[4,8192]{1,0:T(4,128)(2,1)S(1)}, bf16[4,8192]{1,0:T(4,128)(2,1)S(1)}, u32[]{:S(2)}, u32[]{:S(2)}) collective-permute-start(bf16[4,8192]{1,0:T(4,128)(2,1)S(1)} %copy.160), channel_id=1, source_target_pairs={{0,1},{1,2},{2,3},{3,4},{4,5},{5,6},{6,7},{7,8},{8,9},{9,10},{10,1... | collective-permute-start | bytes 196616 | tf_op jit(solution)/shard_map/while/body/eval_jaxpr/ppermute | solution.py:14
  244.6 7.9 %collective-permute-start.1 = (f32[4,8192]{1,0:T(4,128)S(1)}, f32[4,8192]{1,0:T(4,128)S(1)}, u32[]{:S(2)}, u32[]{:S(2)}) collective-permute-start(f32[4,8192]{1,0:T(4,128)S(1)} %fusion.72), channel_id=1, source_target_pairs={{0,1},{1,2},{2,3},{3,4},{4,5},{5,6},{6,7},{7,8},{8,9},{9,10},{10,1... | collective-permute-start | bytes 393224 | tf_op jit(solution)/shard_map/while/body/eval_jaxpr/ppermute | solution.py:14
  (58 other events, 348.8 us)
